TPU v7x, 32 devices: a whole 2x2x4 slice. The times are simulated.
32 devices in a mesh: shard: 2 (over y), ctx: 4 (over z), tp: 4 (over x, core).
Axes of the slice: x: 2, y: 2, z: 4, core: 2. Of those that a mesh axis runs over, the one named last changes fastest.
Arguments:
- inputs: bfloat16 [4, 1024, 768], P('shard', ('ctx', 'tp')), may hold values from -6 to 6
- seg_ids: int32 [4, 1024], P('shard', 'ctx'), may hold values from 0 to 7, never falling along the last dimension, each value on 1 to 512 neighbouring positions
- feature_map: float32 [12, 64, 256], P('tp'), may hold values from -6 to 6
- w_query: bfloat16 [768, 768], P(('shard', 'ctx'), 'tp'), may hold values from -0.21875 to 0.21875
- w_key: bfloat16 [768, 768], P(('shard', 'ctx'), 'tp'), may hold values from -0.21875 to 0.21875
- w_value: bfloat16 [768, 768], P(('shard', 'ctx'), 'tp'), may hold values from -0.21875 to 0.21875
- w_out: bfloat16 [768, 768], P('tp', ('shard', 'ctx')), may hold values from -0.875 to 0.875
- gain_attn: float32 [768], replicated, may hold values from 0.5 to 1.5
- shift_attn: float32 [768], replicated, may hold values from -3 to 3
- w_up: bfloat16 [768, 3072], P(('shard', 'ctx'), 'tp'), may hold values from -0.21875 to 0.21875
- bias_up: float32 [3072], P('tp'), may hold values from -3 to 3
- w_down: bfloat16 [3072, 768], P('tp', ('shard', 'ctx')), may hold values from -0.109375 to 0.109375
- bias_down: float32 [768], replicated, may hold values from -3 to 3
- gain_ffn: float32 [768], replicated, may hold values from 0.5 to 1.5
- shift_ffn: float32 [768], replicated, may hold values from -3 to 3
- cotangent: bfloat16 [4, 1024, 768], P('shard', ('ctx', 'tp')), may hold values from -6 to 6
Outputs:
- outputs: bfloat16 [4, 1024, 768], P('shard', ('ctx', 'tp'))
- grad_inputs: bfloat16 [4, 1024, 768], P('shard', ('ctx', 'tp'))
- grad_query: float32 [768, 768], P(('shard', 'ctx'), 'tp')
- grad_key: float32 [768, 768], P(('shard', 'ctx'), 'tp')
- grad_value: float32 [768, 768], P(('shard', 'ctx'), 'tp')
- grad_out: float32 [768, 768], P('tp', ('shard', 'ctx'))
- grad_gain_attn: float32 [768], replicated
- grad_shift_attn: float32 [768], replicated
- grad_up: float32 [768, 3072], P(('shard', 'ctx'), 'tp')
- grad_bias_up: float32 [3072], P('tp')
- grad_down: float32 [3072, 768], P('tp', ('shard', 'ctx'))
- grad_bias_down: float32 [768], replicated
- grad_gain_ffn: float32 [768], replicated
- grad_shift_ffn: float32 [768], replicated
Inputs may be any that keep to these rules, and one draw needn't show every extreme that they name: `seg_ids`: within each sequence the numbers never fall, every number below 8 occurs, and no document has more than 512 tokens.
All inputs are finite; a program needn't handle non-finite values.
Results may differ from a plain program's by a relative error of at most 0.025.
Values may be sent and summed in bfloat16 or wider, within the bound.
A program may use at most 128 MiB of HBM per device.

v0:
```python
import jax
import jax.numpy as jnp
from jax import lax
from jax.sharding import PartitionSpec as P

HEAD_DIM = 64
FEATS = 256
FF = 3072
SEGS = 8
highest = lax.Precision.HIGHEST
root_half = 0.7071067811865476
inv_root_tau = 0.3989422804014327
norm_eps = 1e-05


def gelu_value(upper):
    return upper * 0.5 * (1.0 + lax.erf(upper * root_half))


def gelu_slope(upper):
    return 0.5 * (1.0 + lax.erf(upper * root_half)) + upper * inv_root_tau * jnp.exp(
        -0.5 * upper * upper
    )


def layer_norm(hidden_in, gain_vec, shift_vec):
    mean_val = jnp.mean(hidden_in, -1, keepdims=True)
    centred = hidden_in - mean_val
    inv_std = lax.rsqrt(jnp.mean(centred * centred, -1, keepdims=True) + norm_eps)
    normed = centred * inv_std
    return (normed * gain_vec + shift_vec, normed, inv_std)


def norm_back(grad_in, normed, inv_std, gain_vec):
    scaled = grad_in * gain_vec
    grad_hidden = inv_std * (
        scaled
        - jnp.mean(scaled, -1, keepdims=True)
        - normed * jnp.mean(scaled * normed, -1, keepdims=True)
    )
    return (grad_hidden, jnp.sum(grad_in * normed, (0, 1)), jnp.sum(grad_in, (0, 1)))


def features(projected, omega_local):
    seq_count, ctx_rows, width = projected.shape
    heads_here = omega_local.shape[0]
    scaled = projected.reshape(seq_count, ctx_rows, heads_here, HEAD_DIM) * HEAD_DIM ** (-0.25)
    angles = jnp.einsum("schd,hdm->schm", scaled, omega_local, precision=highest)
    squares = 0.5 * jnp.sum(scaled * scaled, -1, keepdims=True)
    return (jnp.exp(angles - squares) * FEATS ** (-0.5), scaled)


def feature_back(grad_phi, phi_full, scaled, omega_local):
    grad_angle = grad_phi * phi_full
    grad_scaled = jnp.einsum("schm,hdm->schd", grad_angle, omega_local, precision=highest)
    grad_scaled = grad_scaled - scaled * jnp.sum(grad_angle, -1, keepdims=True)
    seq_count, ctx_rows, heads_here, head_width = scaled.shape
    return (grad_scaled * HEAD_DIM ** (-0.25)).reshape(seq_count, ctx_rows, heads_here * head_width)


def spread_rows(mask_low, left):
    ctx_rows, heads_here, feat_count = left.shape
    wide = mask_low[:, None, :, None] * left[:, :, None, :]
    return wide.reshape(ctx_rows, heads_here, -1)


def segment_outer(operands):
    mask_low, left, right = operands
    return jnp.einsum(
        "chx,che->hxe", spread_rows(mask_low, left), right, preferred_element_type=jnp.float32
    )


def segment_apply(operands):
    mask_low, left, table = operands
    return jnp.einsum(
        "chx,hxe->che", spread_rows(mask_low, left), table, preferred_element_type=jnp.float32
    )


def segment_back(operands):
    mask_full, left, table = operands
    ctx_rows, heads_here, width = left.shape
    seg_count = mask_full.shape[1]
    wide = jnp.einsum("che,hxe->chx", left, table, preferred_element_type=jnp.float32)
    wide = wide.reshape(ctx_rows, heads_here, seg_count, -1)
    return jnp.sum(wide * mask_full[:, None, :, None], 2)


def inner_product(left, right):
    return lax.dot_general(
        left, right, (((0,), (0,)), ((), ())), preferred_element_type=jnp.float32
    )


def right_transposed(left, right):
    return lax.dot_general(
        left, right, (((1,), (1,)), ((), ())), preferred_element_type=jnp.float32
    )


def per_device(
    inputs,
    seg_ids,
    feature_map,
    w_query,
    w_key,
    w_value,
    w_out,
    gain_attn,
    shift_attn,
    w_up,
    bias_up,
    w_down,
    bias_down,
    gain_ffn,
    shift_ffn,
    cotangent,
):
    full_query, full_key, full_value, full_up, full_out, full_down = (
        lax.all_gather(w_query, ("shard", "ctx"), axis=0, tiled=True),
        lax.all_gather(w_key, ("shard", "ctx"), axis=0, tiled=True),
        lax.all_gather(w_value, ("shard", "ctx"), axis=0, tiled=True),
        lax.all_gather(w_up, ("shard", "ctx"), axis=0, tiled=True),
        lax.all_gather(w_out, ("shard", "ctx"), axis=1, tiled=True),
        lax.all_gather(w_down, ("shard", "ctx"), axis=1, tiled=True),
    )
    seq_count, row_share, width = inputs.shape
    rows_all = lax.all_gather(inputs, "tp", axis=1, tiled=True)
    ctx_rows = rows_all.shape[1]
    token_count = seq_count * ctx_rows
    flat = rows_all.reshape(token_count, width)
    heads_here = feature_map.shape[0]
    head_cols = heads_here * HEAD_DIM
    query_proj = jnp.dot(flat, full_query, preferred_element_type=jnp.float32).reshape(
        seq_count, ctx_rows, head_cols
    )
    key_proj = jnp.dot(flat, full_key, preferred_element_type=jnp.float32).reshape(
        seq_count, ctx_rows, head_cols
    )
    value_low = jnp.dot(flat, full_value, preferred_element_type=jnp.float32).astype(jnp.bfloat16)
    value_low = value_low.reshape(seq_count, ctx_rows, head_cols)
    value_four = value_low.reshape(seq_count, ctx_rows, heads_here, HEAD_DIM)
    phi_query, scaled_query = features(query_proj, feature_map)
    phi_key, scaled_key = features(key_proj, feature_map)
    phq_low = phi_query.astype(jnp.bfloat16)
    phk_low = phi_key.astype(jnp.bfloat16)
    matches = seg_ids[:, :, None] == jnp.arange(SEGS, dtype=jnp.int32)[None, None, :]
    mask_low = matches.astype(jnp.bfloat16)
    mask_full = matches.astype(jnp.float32)
    kv_part = lax.map(segment_outer, (mask_low, phk_low, value_four))
    z_part = jnp.einsum("scg,schm->shgm", mask_low, phk_low, preferred_element_type=jnp.float32)
    kv_sum, z_sum = lax.psum((kv_part, z_part), "ctx")
    kv_low = kv_sum.astype(jnp.bfloat16)
    numer = lax.map(segment_apply, (mask_low, phq_low, kv_low))
    phq_wide = phq_low.astype(jnp.float32)
    denom = jnp.sum(
        jnp.einsum("schm,shgm->schg", phq_wide, z_sum, precision=highest)
        * mask_full[:, :, None, :],
        -1,
    )
    mixed = numer / denom[..., None]
    mixed_low = mixed.astype(jnp.bfloat16).reshape(seq_count, ctx_rows, head_cols)
    piece = mixed_low
    attn_sum = jnp.swapaxes(
        lax.psum_scatter(
            jnp.einsum("scf,fd->csd", piece, full_out, preferred_element_type=jnp.float32),
            "tp",
            scatter_dimension=0,
            tiled=True,
        ),
        0,
        1,
    )
    first, normed_one, inv_one = layer_norm(
        inputs.astype(jnp.float32) + attn_sum, gain_attn, shift_attn
    )
    first_low = first.astype(jnp.bfloat16)
    first_rows = lax.all_gather(first_low, "tp", axis=1, tiled=True)
    first_flat = first_rows.reshape(token_count, width)
    upper = jnp.dot(first_flat, full_up, preferred_element_type=jnp.float32) + bias_up
    ffn_here = upper.shape[1]
    hidden_low = gelu_value(upper).astype(jnp.bfloat16)
    hidden_three = hidden_low.reshape(seq_count, ctx_rows, ffn_here)
    piece = hidden_three
    branch = jnp.swapaxes(
        lax.psum_scatter(
            jnp.einsum("scf,fd->csd", piece, full_down, preferred_element_type=jnp.float32),
            "tp",
            scatter_dimension=0,
            tiled=True,
        ),
        0,
        1,
    )
    final, normed_two, inv_two = layer_norm(first + branch + bias_down, gain_ffn, shift_ffn)
    outputs = final.astype(jnp.bfloat16)
    full_query, full_key, full_value, full_up, full_out, full_down = (
        lax.all_gather(w_query, ("shard", "ctx"), axis=0, tiled=True),
        lax.all_gather(w_key, ("shard", "ctx"), axis=0, tiled=True),
        lax.all_gather(w_value, ("shard", "ctx"), axis=0, tiled=True),
        lax.all_gather(w_up, ("shard", "ctx"), axis=0, tiled=True),
        lax.all_gather(w_out, ("shard", "ctx"), axis=1, tiled=True),
        lax.all_gather(w_down, ("shard", "ctx"), axis=1, tiled=True),
    )
    grad_final = cotangent.astype(jnp.float32)
    grad_two, grad_gain_ffn, grad_shift_ffn = norm_back(grad_final, normed_two, inv_two, gain_ffn)
    grad_bias_down = jnp.sum(grad_two, (0, 1))
    grad_two_rows = lax.all_gather(grad_two.astype(jnp.bfloat16), "tp", axis=1, tiled=True)
    grad_two_flat = grad_two_rows.reshape(token_count, width)
    grad_hidden = right_transposed(grad_two_flat, full_down)
    grad_upper = (grad_hidden * gelu_slope(upper)).astype(jnp.bfloat16)
    grad_down = inner_product(hidden_low, grad_two_flat)
    grad_up = inner_product(first_flat, grad_upper)
    grad_bias_local = jnp.sum(grad_upper.astype(jnp.float32), 0)
    grad_upper_three = grad_upper.reshape(seq_count, ctx_rows, ffn_here)
    piece = grad_upper_three
    grad_first = grad_two + jnp.swapaxes(
        lax.psum_scatter(
            jnp.einsum("scf,df->csd", piece, full_up, preferred_element_type=jnp.float32),
            "tp",
            scatter_dimension=0,
            tiled=True,
        ),
        0,
        1,
    )
    grad_one, grad_gain_attn, grad_shift_attn = norm_back(
        grad_first, normed_one, inv_one, gain_attn
    )
    grad_one_rows = lax.all_gather(grad_one.astype(jnp.bfloat16), "tp", axis=1, tiled=True)
    grad_one_flat = grad_one_rows.reshape(token_count, width)
    grad_out = inner_product(mixed_low.reshape(token_count, head_cols), grad_one_flat)
    grad_mixed = right_transposed(grad_one_flat, full_out).reshape(
        seq_count, ctx_rows, heads_here, HEAD_DIM
    )
    grad_numer = (grad_mixed / denom[..., None]).astype(jnp.bfloat16)
    grad_denom = -jnp.sum(grad_mixed * mixed, -1) / denom
    kv_grad_part = lax.map(segment_outer, (mask_low, phq_low, grad_numer))
    z_grad_part = jnp.einsum(
        "scg,schm->shgm", mask_full, phq_wide * grad_denom[..., None], precision=highest
    )
    kv_grad, z_grad = (
        lax.psum(kv_grad_part.astype(jnp.bfloat16), "ctx").astype(jnp.float32),
        lax.psum(z_grad_part.astype(jnp.bfloat16), "ctx").astype(jnp.float32),
    )
    kv_grad_low = kv_grad.astype(jnp.bfloat16)
    grad_phq = lax.map(segment_back, (mask_full, grad_numer, kv_low))
    grad_phq = grad_phq + grad_denom[..., None] * jnp.einsum(
        "scg,shgm->schm", mask_full, z_sum, precision=highest
    )
    grad_phk = lax.map(segment_back, (mask_full, value_four, kv_grad_low))
    grad_phk = grad_phk + jnp.einsum("scg,shgm->schm", mask_full, z_grad, precision=highest)
    grad_value_rows = lax.map(segment_apply, (mask_low, phk_low, kv_grad_low)).astype(jnp.bfloat16)
    grad_value_rows = grad_value_rows.reshape(seq_count, ctx_rows, head_cols)
    grad_query_rows = feature_back(grad_phq, phi_query, scaled_query, feature_map).astype(
        jnp.bfloat16
    )
    grad_key_rows = feature_back(grad_phk, phi_key, scaled_key, feature_map).astype(jnp.bfloat16)
    grad_query = inner_product(flat, grad_query_rows.reshape(token_count, head_cols))
    grad_key = inner_product(flat, grad_key_rows.reshape(token_count, head_cols))
    grad_value = inner_product(flat, grad_value_rows.reshape(token_count, head_cols))
    total = jnp.einsum(
        "scf,df->csd", grad_query_rows, full_query, preferred_element_type=jnp.float32
    )
    total = total + jnp.einsum(
        "scf,df->csd", grad_key_rows, full_key, preferred_element_type=jnp.float32
    )
    grad_rows = jnp.swapaxes(
        lax.psum_scatter(
            (
                total
                + jnp.einsum(
                    "scf,df->csd", grad_value_rows, full_value, preferred_element_type=jnp.float32
                )
            ).astype(jnp.bfloat16),
            "tp",
            scatter_dimension=0,
            tiled=True,
        ).astype(jnp.float32),
        0,
        1,
    )
    grad_inputs = (grad_one + grad_rows).astype(jnp.bfloat16)
    grad_query, grad_key, grad_value, grad_up, grad_out, grad_down = (
        lax.psum_scatter(grad_query, ("shard", "ctx"), scatter_dimension=0, tiled=True),
        lax.psum_scatter(grad_key, ("shard", "ctx"), scatter_dimension=0, tiled=True),
        lax.psum_scatter(grad_value, ("shard", "ctx"), scatter_dimension=0, tiled=True),
        lax.psum_scatter(grad_up, ("shard", "ctx"), scatter_dimension=0, tiled=True),
        lax.psum_scatter(grad_out, ("shard", "ctx"), scatter_dimension=1, tiled=True),
        lax.psum_scatter(grad_down, ("shard", "ctx"), scatter_dimension=1, tiled=True),
    )
    tp_index = lax.axis_index("tp")
    padded_bias = lax.dynamic_update_slice(
        jnp.zeros((FF,), jnp.float32), grad_bias_local, (tp_index * ffn_here,)
    )
    grad_gain_attn, grad_shift_attn, grad_gain_ffn, grad_shift_ffn, grad_bias_down, padded_bias = (
        lax.psum(
            (
                grad_gain_attn,
                grad_shift_attn,
                grad_gain_ffn,
                grad_shift_ffn,
                grad_bias_down,
                padded_bias,
            ),
            ("shard", "ctx", "tp"),
        )
    )
    grad_bias_up = lax.dynamic_slice(padded_bias, (tp_index * ffn_here,), (ffn_here,))
    return (
        outputs,
        grad_inputs,
        grad_query,
        grad_key,
        grad_value,
        grad_out,
        grad_gain_attn,
        grad_shift_attn,
        grad_up,
        grad_bias_up,
        grad_down,
        grad_bias_down,
        grad_gain_ffn,
        grad_shift_ffn,
    )


def solution(mesh):
    placed = (
        P("shard", ("ctx", "tp"), None),
        P("shard", "ctx"),
        P("tp", None, None),
        P(("shard", "ctx"), "tp"),
        P(("shard", "ctx"), "tp"),
        P(("shard", "ctx"), "tp"),
        P("tp", ("shard", "ctx")),
        P(),
        P(),
        P(("shard", "ctx"), "tp"),
        P("tp"),
        P("tp", ("shard", "ctx")),
        P(),
        P(),
        P(),
        P("shard", ("ctx", "tp"), None),
    )
    return jax.shard_map(
        per_device,
        mesh=mesh,
        in_specs=placed,
        out_specs=(
            P("shard", ("ctx", "tp"), None),
            P("shard", ("ctx", "tp"), None),
            P(("shard", "ctx"), "tp"),
            P(("shard", "ctx"), "tp"),
            P(("shard", "ctx"), "tp"),
            P("tp", ("shard", "ctx")),
            P(),
            P(),
            P(("shard", "ctx"), "tp"),
            P("tp"),
            P("tp", ("shard", "ctx")),
            P(),
            P(),
            P(),
        ),
        check_vma=False,
    )
```

profile of v0, /device:TPU:0, one launch (start us, length us, event | category | flops | bytes accessed | tf_op | source)
XLA Modules:
  0.0 1010.8 jit_solution(17872332154931087539)
XLA Ops:
  8.1 10.4 %all_gather.36 = bf16[2,256,768]{2,1,0:T(8,128)(2,1)S(1)} all-gather(bf16[2,64,768]{2,1,0:T(8,128)(2,1)} %param.28), channel_id=1, replica_groups=mesh['shard'=2,'ctx'=4,'tp'=4] {'tp'}, dimensions={1}, use_global_device_ids=true | all-gather | bytes 983040 | tf_op jit(solution)/shard_map/all_gather | solution.py:129
  18.5 32.5 %all_gather.37 = bf16[768,192]{1,0:T(8,128)(2,1)S(1)} all-gather(bf16[96,192]{1,0:T(8,128)(2,1)} %param.32), channel_id=1, replica_groups=mesh['shard'=2,'ctx'=4,'tp'=4] {'shard','ctx'}, dimensions={0}, use_global_device_ids=true | all-gather | bytes 331776 | tf_op jit(solution)/shard_map/all_gather | solution.py:122
  52.3 2.7 fusion.159
  56.2 31.6 %all_gather.38 = bf16[768,192]{1,0:T(8,128)(2,1)S(1)} all-gather(bf16[96,192]{1,0:T(8,128)(2,1)S(1)} %copy-done.48), channel_id=1, replica_groups=mesh['shard'=2,'ctx'=4,'tp'=4] {'shard','ctx'}, dimensions={0}, use_global_device_ids=true | all-gather | bytes 331776 | tf_op jit(solution)/shard_map/all_gather | solution.py:123
  90.6 2.1 convolution_bitcast_fusion.8
  92.7 20.8 %while.66 = (s32[]{:T(128)}, f32[2,3,2048,64]{2,3,1,0:T(8,128)}, bf16[2,256,8]{2,1,0:T(8,128)(2,1)S(1)}, bf16[2,256,3,256]{3,1,2,0:T(8,128)(2,1)}, bf16[2,256,3,64]{1,3,2,0:T(8,128)(2,1)}) while((s32[]{:T(128)}, f32[2,3,2048,64]{2,3,1,0:T(8,128)}, bf16[2,256,8]{2,1,0:T(8,128)(2,1)S(1)}, bf16[2,256,3,256]{3,1,2,0:T(8,128)(2,1)}, ...), condition=%wide.region_3.4_spmd.clone, body=%wide.region_2.3_spmd.sunk.clone | while | flops 207618048 | bytes 20427872 | solution.py:151
  93.7 2.2 mul.739
  95.9 4.2 mul.740
  101.1 2.1 fusion.233
  104.2 2.2 mul.739
  106.4 4.2 mul.740
  111.5 2.0 fusion.233
  113.6 32.0 %all_gather.39 = bf16[768,192]{1,0:T(8,128)(2,1)S(1)} all-gather(bf16[96,192]{1,0:T(8,128)(2,1)S(1)} %copy-done.49), channel_id=1, replica_groups=mesh['shard'=2,'ctx'=4,'tp'=4] {'shard','ctx'}, dimensions={0}, use_global_device_ids=true | all-gather | bytes 331776 | tf_op jit(solution)/shard_map/all_gather | solution.py:121
  145.7 2.3 broadcast_multiply_fusion
  148.0 2.7 fusion.160
  152.0 96.4 %all-reduce.6 = (bf16[2,3,2048,64]{2,3,1,0:T(8,128)(2,1)}, f32[2,3,8,256]{3,2,1,0:T(8,128)S(1)}) all-reduce(f32[2,3,2048,64]{2,3,1,0:T(8,128)} %get-tuple-element.176, f32[2,3,8,256]{3,2,1,0:T(8,128)S(1)} %copy-done.46), channel_id=1, replica_groups=mesh['shard'=2,'ctx'=4,'tp'=4] {'ctx'}, use_global_device_ids=true, to_apply=%region_4.5 | all-reduce | flops 798720 | bytes 4816896 | tf_op jit(solution)/shard_map/psum | solution.py:153
  248.4 19.4 %while.67 = (s32[]{:T(128)}, f32[2,256,3,64]{1,3,2,0:T(8,128)}, bf16[2,3,2048,64]{2,3,1,0:T(8,128)(2,1)}, bf16[2,256,8]{2,1,0:T(8,128)(2,1)S(1)}, bf16[2,256,3,256]{3,1,2,0:T(8,128)(2,1)}) while((s32[]{:T(128)}, f32[2,256,3,64]{1,3,2,0:T(8,128)}, bf16[2,3,2048,64]{2,3,1,0:T(8,128)(2,1)}, bf16[2,256,8]{2,1,0:T(8,128)(2,1)S(1)}, ...), condition=%wide.region_6.7_spmd.clone, body=%wide.region_5.6_spmd.sunk.clone | while | flops 202899456 | bytes 31536224 | solution.py:155
  249.9 3.5 mul.745
  255.2 2.9 fusion.236
  259.6 3.5 mul.745
  264.9 2.9 fusion.236
  268.7 31.8 %all_gather.40 = bf16[192,768]{0,1:T(8,128)(2,1)S(1)} all-gather(bf16[192,96]{0,1:T(8,128)(2,1)S(1)} %copy.105), channel_id=1, replica_groups=mesh['shard'=2,'ctx'=4,'tp'=4] {'shard','ctx'}, dimensions={1}, use_global_device_ids=true | all-gather | bytes 331776 | tf_op jit(solution)/shard_map/all_gather | solution.py:125
  300.6 1.9 fusion.106
  305.4 27.2 %reduce-scatter.19.cloned.1.call-done = f32[64,2,768]{2,0,1:T(8,128)} async-done(((f32[256,2,768]{2,0,1:T(8,128)}), f32[64,2,768]{2,0,1:T(8,128)}) %reduce-scatter.19.cloned.1.call-update) | async-done | bytes 393232 | tf_op jit(solution)/shard_map/reduce_scatter | solution.py:166
  334.7 8.0 all_gather.41
  342.7 5.8 all-gather.3.cloned.1.call-done
  348.4 3.3 multiply_convert_fusion
  351.7 38.5 %all-gather.5.cloned.1.call-done = bf16[768,768]{0,1:T(8,128)(2,1)} async-done(((bf16[768,96]{0,1:T(8,128)(2,1)}), bf16[768,768]{0,1:T(8,128)(2,1)}) %all-gather.5.cloned.1.call-update) | async-done | bytes 1179664 | tf_op jit(solution)/shard_map/all_gather | solution.py:126
  390.2 3.3 convolution_bitcast_fusion.2
  393.6 26.5 %reduce-scatter.21.cloned.1.call-done = f32[64,2,768]{2,0,1:T(8,128)} async-done(((f32[256,2,768]{2,0,1:T(8,128)}), f32[64,2,768]{2,0,1:T(8,128)}) %reduce-scatter.21.cloned.1.call-update) | async-done | bytes 393232 | tf_op jit(solution)/shard_map/reduce_scatter | solution.py:187
  422.0 8.1 all_gather.44
  432.7 2.0 convolution_bitcast_fusion.1
  438.0 25.5 %reduce-scatter.23.cloned.1.call-done = f32[64,2,768]{2,0,1:T(8,128)} async-done(((f32[256,2,768]{2,0,1:T(8,128)}), f32[64,2,768]{2,0,1:T(8,128)}) %reduce-scatter.23.cloned.1.call-update) | async-done | bytes 393232 | tf_op jit(solution)/shard_map/reduce_scatter | solution.py:219
  463.5 2.7 fusion.122
  466.4 8.0 all_gather.45
  476.2 20.0 %while.69 = (s32[]{:T(128)}, bf16[2,3,2048,64]{2,3,1,0:T(8,128)(2,1)}, bf16[2,256,8]{2,1,0:T(8,128)(2,1)S(1)}, bf16[2,256,3,256]{3,1,2,0:T(8,128)(2,1)}, bf16[2,256,3,64]{1,3,2,0:T(8,128)(2,1)}) while((s32[]{:T(128)}, bf16[2,3,2048,64]{2,3,1,0:T(8,128)(2,1)}, bf16[2,256,8]{2,1,0:T(8,128)(2,1)S(1)}, ...), condition=%wide.region_26.27_spmd.clone, body=%wide.region_25.26_spmd.sunk.clone | while | flops 207618048 | bytes 20427872 | solution.py:239
  477.2 2.1 mul.751
  479.2 4.2 mul.752
  487.2 2.1 mul.751
  489.2 4.2 mul.752
  497.8 7.0 while.68
  497.8 2.0 fusion.239
  501.3 1.9 fusion.239
  504.8 2.5 fusion.161
  508.3 20.2 %psum.73 = bf16[2,3,8,256]{3,2,1,0:T(8,128)(2,1)S(1)} all-reduce(bf16[2,3,8,256]{3,2,1,0:T(8,128)(2,1)S(1)} %fusion.107), channel_id=1, replica_groups=mesh['shard'=2,'ctx'=4,'tp'=4] {'ctx'}, use_global_device_ids=true, to_apply=%region_31.32 | all-reduce | flops 12288 | bytes 49152 | tf_op jit(solution)/shard_map/psum | solution.py:245
  532.7 33.9 %all-reduce.5.cloned.1.call-done = bf16[2,3,2048,64]{2,3,1,0:T(8,128)(2,1)} async-done(((bf16[2,3,2048,64]{2,3,1,0:T(8,128)(2,1)}), bf16[2,3,2048,64]{2,3,1,0:T(8,128)(2,1)}) %all-reduce.5.cloned.1.call-update) | async-done | bytes 1572880 | tf_op jit(solution)/shard_map/psum | solution.py:244
  568.0 7.5 while.70
  568.0 2.3 fusion.245
  571.8 2.2 fusion.245
  575.5 2.0 fusion.162
  580.4 19.7 %while.71 = (s32[]{:T(128)}, bf16[2,256,3,64]{1,3,2,0:T(8,128)(2,1)}, bf16[2,3,2048,64]{2,3,1,0:T(8,128)(2,1)}, bf16[2,256,8]{2,1,0:T(8,128)(2,1)S(1)}, bf16[2,256,3,256]{3,1,2,0:T(8,128)(2,1)}) while((s32[]{:T(128)}, bf16[2,256,3,64]{1,3,2,0:T(8,128)(2,1)}, bf16[2,3,2048,64]{2,3,1,0:T(8,128)(2,1)}, ...), condition=%wide.region_34.35_spmd.clone, body=%wide.region_33.34_spmd.sunk.clone | while | flops 202899456 | bytes 33109144 | solution.py:254
  581.9 3.5 mul.759
  587.4 2.2 fusion.248
  591.7 3.5 mul.759
  597.2 2.2 fusion.248
  600.1 3.5 fusion.75
  605.5 2.2 fusion.164
  609.1 2.2 fusion.163
  616.1 40.8 %all-reduce = (f32[768]{0:T(1024)}, f32[768]{0:T(1024)}, f32[3072]{0:T(1024)S(1)}, f32[768]{0:T(1024)}, f32[768]{0:T(1024)}, /*index=5*/f32[768]{0:T(1024)}) all-reduce(f32[768]{0:T(1024)S(1)} %copy-done.69, f32[768]{0:T(1024)S(1)} %copy-done.68, ...), channel_id=1, replica_groups=mesh['shard'=2,'ctx'=4,'tp'=4] {'shard','ctx','tp'}, use_global_device_ids=true, to_apply=%region_41.42 | all-reduce | flops 6912 | bytes 55296 | tf_op jit(solution)/shard_map/psum | solution.py:298
  661.1 63.8 %reduce-scatter.31.cloned.1.call-done = f32[96,192]{1,0:T(8,128)} async-done(((f32[768,192]{1,0:T(8,128)}), f32[96,192]{1,0:T(8,128)}) %reduce-scatter.31.cloned.1.call-update) | async-done | bytes 73744
  724.9 73.0 %reduce-scatter.29.cloned.1.call-done = f32[768,96]{0,1:T(8,128)} async-done(((f32[768,768]{0,1:T(8,128)}), f32[768,96]{0,1:T(8,128)}) %reduce-scatter.29.cloned.1.call-update) | async-done | bytes 294928 | tf_op jit(solution)/shard_map/reduce_scatter | solution.py:291
  797.9 73.1 %reduce-scatter.27.cloned.1.call-done = f32[96,768]{1,0:T(8,128)} async-done(((f32[768,768]{1,0:T(8,128)}), f32[96,768]{1,0:T(8,128)}) %reduce-scatter.27.cloned.1.call-update) | async-done | bytes 294928 | tf_op jit(solution)/shard_map/reduce_scatter | solution.py:289
  871.0 66.2 %reduce-scatter.33.cloned.1.call-done = f32[96,192]{1,0:T(8,128)} async-done(((f32[768,192]{1,0:T(8,128)}), f32[96,192]{1,0:T(8,128)}) %reduce-scatter.33.cloned.1.call-update) | async-done | bytes 73744
  937.2 66.2 %reduce-scatter.35.cloned.1.call-done = f32[96,192]{1,0:T(8,128)} async-done(((f32[768,192]{1,0:T(8,128)}), f32[96,192]{1,0:T(8,128)}) %reduce-scatter.35.cloned.1.call-update) | async-done | bytes 73744
  (326 shorter events, 77.2 us)
Async XLA Ops:
  8.0 44.3 %copy-start = (f32[3,64,256]{2,1,0:T(8,128)S(1)}, f32[3,64,256]{2,1,0:T(8,128)}, u32[]{:S(2)}) copy-start(f32[3,64,256]{2,1,0:T(8,128)} %param.30) | copy-start | bytes 589828
  8.0 324.6 %reduce-scatter.19.cloned.1.call-start = ((), (), s32[]{:S(2)}) async-start(), calls=%async_computation.10 | async-start | bytes 1966080 | tf_op jit(solution)/shard_map/reduce_scatter | solution.py:166
  18.5 69.3 %copy-start.4 = (bf16[2,256,768]{2,1,0:T(8,128)(2,1)}, bf16[2,256,768]{2,1,0:T(8,128)(2,1)S(1)}, u32[]{:S(2)}) copy-start(bf16[2,256,768]{2,1,0:T(8,128)(2,1)S(1)} %all_gather.36) | copy-start | bytes 2359300
  51.0 4.1 copy-start.16
  52.3 3.9 copy-start.48
  56.2 33.5 %copy-start.56 = (s32[2,256]{1,0:T(2,128)S(1)}, s32[2,256]{1,0:T(2,128)}, u32[]{:S(2)}) copy-start(s32[2,256]{1,0:T(2,128)} %param.29) | copy-start | bytes 6148
  92.7 20.8 %copy-start.49 = (bf16[96,192]{1,0:T(8,128)(2,1)S(1)}, bf16[96,192]{1,0:T(8,128)(2,1)}, u32[]{:S(2)}) copy-start(bf16[96,192]{1,0:T(8,128)(2,1)} %param.31) | copy-start | bytes 110596
  145.5 5.2 copy-start.18
  148.0 3.9 copy-start.40
  150.7 97.6 %copy-start.24 = (bf16[2,256,3,256]{1,3,0,2:T(8,128)(2,1)}, bf16[2,256,3,256]{1,3,0,2:T(8,128)(2,1)S(1)}, u32[]{:S(2)}) copy-start(bf16[2,256,3,256]{1,3,0,2:T(8,128)(2,1)S(1)} %get-tuple-element.414) | copy-start | bytes 2359300
  267.8 34.6 %copy-start.45 = (f32[2,256,3,64]{1,3,2,0:T(8,128)S(1)}, f32[2,256,3,64]{1,3,2,0:T(8,128)}, u32[]{:S(2)}) copy-start(f32[2,256,3,64]{1,3,2,0:T(8,128)} %get-tuple-element.177) | copy-start | bytes 1179652
  302.5 30.1 %copy-start.42 = (bf16[2,64,768]{2,1,0:T(8,128)(2,1)S(1)}, bf16[2,64,768]{2,1,0:T(8,128)(2,1)}, u32[]{:S(2)}) copy-start(bf16[2,64,768]{2,1,0:T(8,128)(2,1)} %param.28) | copy-start | bytes 589828
  304.1 30.4 %copy-start.47 = (f32[768]{0:T(1024)S(1)}, f32[768]{0:T(1024)}, u32[]{:S(2)}) copy-start(f32[768]{0:T(1024)} %param.35) | copy-start | bytes 9220
  304.1 30.4 %copy-start.61 = (f32[768]{0:T(1024)S(1)}, f32[768]{0:T(1024)}, u32[]{:S(2)}) copy-start(f32[768]{0:T(1024)} %param.36) | copy-start | bytes 9220
  304.1 44.3 %all-gather.3.cloned.1.call-start = ((), (), s32[]{:S(2)}) async-start(), calls=%async_computation.11 | async-start | bytes 1327104 | tf_op jit(solution)/shard_map/all_gather | solution.py:124
  304.7 85.5 %all-gather.5.cloned.1.call-start = ((), (), s32[]{:S(2)}) async-start(), calls=%async_computation.12 | async-start | bytes 1327104 | tf_op jit(solution)/shard_map/all_gather | solution.py:126
  305.3 114.8 %reduce-scatter.21.cloned.1.call-start = ((), (), s32[]{:S(2)}) async-start(), calls=%async_computation.13 | async-start | bytes 1966080 | tf_op jit(solution)/shard_map/reduce_scatter | solution.py:187
  333.7 132.5 %copy-start.6 = (f32[2,64,768]{2,1,0:T(8,128)}, f32[2,64,768]{2,1,0:T(8,128)S(1)}, u32[]{:S(2)}) copy-start(f32[2,64,768]{2,1,0:T(8,128)S(1)} %get-tuple-element.395) | copy-start | bytes 1179652
  342.7 9.0 copy-start.12
  351.7 41.8 %copy-start.28 = (bf16[512,768]{1,0:T(8,128)(2,1)}, bf16[512,768]{1,0:T(8,128)(2,1)S(1)}, u32[]{:S(2)}) copy-start(bf16[512,768]{1,0:T(8,128)(2,1)S(1)} %get-tuple-element.416) | copy-start | bytes 2359300
  393.5 26.6 %copy-start.53 = (f32[2,64]{1,0:T(2,128)S(1)}, f32[2,64]{1,0:T(2,128)}, u32[]{:S(2)}) copy-start(f32[2,64]{1,0:T(2,128)} %copy-done.52) | copy-start | bytes 1540
  393.5 26.6 %copy-start.62 = (f32[768]{0:T(1024)S(1)}, f32[768]{0:T(1024)}, u32[]{:S(2)}) copy-start(f32[768]{0:T(1024)} %param.36) | copy-start | bytes 9220
  393.5 26.6 %copy-start.78 = (f32[768]{0:T(1024)S(1)}, f32[768]{0:T(1024)}, u32[]{:S(2)}) copy-start(f32[768]{0:T(1024)} %param.40) | copy-start | bytes 9220
  393.5 28.1 %copy-start.37 = (bf16[2,64,768]{2,1,0:T(8,128)(2,1)S(1)}, bf16[2,64,768]{2,1,0:T(8,128)(2,1)}, u32[]{:S(2)}) copy-start(bf16[2,64,768]{2,1,0:T(8,128)(2,1)} %param.43) | copy-start | bytes 589828
  393.5 28.1 %copy-start.50 = (f32[768]{0:T(1024)S(1)}, f32[768]{0:T(1024)}, u32[]{:S(2)}) copy-start(f32[768]{0:T(1024)} %param.41) | copy-start | bytes 9220
  393.5 69.9 %reduce-scatter.23.cloned.1.call-start = ((), (), s32[]{:S(2)}) async-start(), calls=%async_computation.14 | async-start | bytes 1966080 | tf_op jit(solution)/shard_map/reduce_scatter | solution.py:219
  421.3 8.8 copy-start.82
  421.3 8.8 copy-start.83
  421.3 10.5 %copy-start.58 = (f32[2,64]{1,0:T(2,128)}, f32[2,64]{1,0:T(2,128)S(1)}, u32[]{:S(2)}) copy-start(f32[2,64]{1,0:T(2,128)S(1)} %broadcast_multiply_fusion.10) | copy-start | bytes 1540
  421.6 10.3 %copy-start.63 = (f32[2,64]{1,0:T(2,128)}, f32[2,64]{1,0:T(2,128)S(1)}, u32[]{:S(2)}) copy-start(f32[2,64]{1,0:T(2,128)S(1)} %add_rsqrt_fusion) | copy-start | bytes 1540
  421.8 10.0 copy-start.70
  421.8 10.0 copy-start.72
  434.8 28.7 %copy-start.51 = (f32[768]{0:T(1024)S(1)}, f32[768]{0:T(1024)}, u32[]{:S(2)}) copy-start(f32[768]{0:T(1024)} %param.41) | copy-start | bytes 9220
  434.8 28.7 %copy-start.54 = (f32[2,64]{1,0:T(2,128)S(1)}, f32[2,64]{1,0:T(2,128)}, u32[]{:S(2)}) copy-start(f32[2,64]{1,0:T(2,128)} %copy-done.52) | copy-start | bytes 1540
  434.8 28.7 %copy-start.59 = (f32[2,64]{1,0:T(2,128)S(1)}, f32[2,64]{1,0:T(2,128)}, u32[]{:S(2)}) copy-start(f32[2,64]{1,0:T(2,128)} %copy-done.58) | copy-start | bytes 1540
  434.8 28.7 %copy-start.64 = (f32[2,64]{1,0:T(2,128)S(1)}, f32[2,64]{1,0:T(2,128)}, u32[]{:S(2)}) copy-start(f32[2,64]{1,0:T(2,128)} %copy-done.63) | copy-start | bytes 1540
  434.8 28.7 %copy-start.71 = (f32[2,64]{1,0:T(2,128)S(1)}, f32[2,64]{1,0:T(2,128)}, u32[]{:S(2)}) copy-start(f32[2,64]{1,0:T(2,128)} %copy-done.70) | copy-start | bytes 1540
  434.8 28.7 %copy-start.73 = (f32[2,64]{1,0:T(2,128)S(1)}, f32[2,64]{1,0:T(2,128)}, u32[]{:S(2)}) copy-start(f32[2,64]{1,0:T(2,128)} %copy-done.72) | copy-start | bytes 1540
  434.8 28.7 %copy-start.79 = (f32[768]{0:T(1024)S(1)}, f32[768]{0:T(1024)}, u32[]{:S(2)}) copy-start(f32[768]{0:T(1024)} %param.42) | copy-start | bytes 9220
  434.8 131.8 %all-reduce.5.cloned.1.call-start = ((), (), s32[]{:S(2)}) async-start(), calls=%async_computation.15 | async-start | bytes 3145728 | tf_op jit(solution)/shard_map/psum | solution.py:244
  466.2 9.3 copy-start.20
  466.2 9.3 copy-start.74
  466.2 9.3 copy-start.76
  496.2 161.4 %reduce-scatter.37.cloned.1.call-start = ((), (), s32[]{:S(2)}) async-start(), calls=%async_computation.22 | async-start | bytes 884736
  497.8 7.0 copy-start.10
  497.8 7.0 copy-start.57
  507.3 21.2 %copy-start.23 = (bf16[2,256,768]{2,1,0:T(8,128)(2,1)S(1)}, bf16[2,256,768]{2,1,0:T(8,128)(2,1)}, u32[]{:S(2)}) copy-start(bf16[2,256,768]{2,1,0:T(8,128)(2,1)} %copy-done.22) | copy-start | bytes 2359300
  507.3 21.2 %copy-start.41 = (bf16[24,8,2,256]{3,1,2,0:T(8,128)(2,1)S(1)}, bf16[24,8,2,256]{3,1,2,0:T(8,128)(2,1)}, u32[]{:S(2)}) copy-start(bf16[24,8,2,256]{3,1,2,0:T(8,128)(2,1)} %copy.197) | copy-start | bytes 589828
  507.4 22.5 %copy-start.39 = (f32[2,256,3,64]{1,3,2,0:T(8,128)S(1)}, f32[2,256,3,64]{1,3,2,0:T(8,128)}, u32[]{:S(2)}) copy-start(f32[2,256,3,64]{1,3,2,0:T(8,128)} %get-tuple-element.413) | copy-start | bytes 1179652
  531.0 37.0 %copy-start.33 = (bf16[2,256,3,64]{1,3,2,0:T(8,128)(2,1)}, bf16[2,256,3,64]{1,3,2,0:T(8,128)(2,1)S(1)}, u32[]{:S(2)}) copy-start(bf16[2,256,3,64]{1,3,2,0:T(8,128)(2,1)S(1)} %fusion.96) | copy-start | bytes 589828
  532.6 35.4 %copy-start.9 = (bf16[2,256,3,64]{1,3,2,0:T(8,128)(2,1)S(1)}, bf16[2,256,3,64]{1,3,2,0:T(8,128)(2,1)}, u32[]{:S(2)}) copy-start(bf16[2,256,3,64]{1,3,2,0:T(8,128)(2,1)} %get-tuple-element.797) | copy-start | bytes 589828
  532.7 126.6 %reduce-scatter.25.cloned.1.call-start = ((), (), s32[]{:S(2)}) async-start(), calls=%async_computation.16 | async-start | bytes 983040 | tf_op jit(solution)/shard_map/reduce_scatter | solution.py:270
  568.0 7.5 copy-start.11
  600.1 3.8 copy-start.34
  603.6 121.3 %reduce-scatter.31.cloned.1.call-start = ((), (), s32[]{:S(2)}) async-start(), calls=%async_computation.19 | async-start | bytes 884736
  605.4 192.4 %reduce-scatter.29.cloned.1.call-start = ((), (), s32[]{:S(2)}) async-start(), calls=%async_computation.18 | async-start | bytes 2654208 | tf_op jit(solution)/shard_map/reduce_scatter | solution.py:291
  607.8 263.2 %reduce-scatter.27.cloned.1.call-start = ((), (), s32[]{:S(2)}) async-start(), calls=%async_computation.17 | async-start | bytes 2654208 | tf_op jit(solution)/shard_map/reduce_scatter | solution.py:289
  611.4 325.8 %reduce-scatter.33.cloned.1.call-start = ((), (), s32[]{:S(2)}) async-start(), calls=%async_computation.20 | async-start | bytes 884736
  613.8 389.6 %reduce-scatter.35.cloned.1.call-start = ((), (), s32[]{:S(2)}) async-start(), calls=%async_computation.21 | async-start | bytes 884736
  614.5 44.8 %copy-start.7 = (f32[2,64,768]{2,1,0:T(8,128)S(1)}, f32[2,64,768]{2,1,0:T(8,128)}, u32[]{:S(2)}) copy-start(f32[2,64,768]{2,1,0:T(8,128)} %copy-done.6) | copy-start | bytes 1179652
  614.5 44.8 %copy-start.21 = (f32[2,64,768]{2,1,0:T(8,128)S(1)}, f32[2,64,768]{2,1,0:T(8,128)}, u32[]{:S(2)}) copy-start(f32[2,64,768]{2,1,0:T(8,128)} %copy-done.20) | copy-start | bytes 1179652
  614.5 44.8 %copy-start.55 = (f32[2,64]{1,0:T(2,128)S(1)}, f32[2,64]{1,0:T(2,128)}, u32[]{:S(2)}) copy-start(f32[2,64]{1,0:T(2,128)} %copy-done.52) | copy-start | bytes 1540
  614.5 44.8 %copy-start.75 = (f32[2,64]{1,0:T(2,128)S(1)}, f32[2,64]{1,0:T(2,128)}, u32[]{:S(2)}) copy-start(f32[2,64]{1,0:T(2,128)} %copy-done.74) | copy-start | bytes 1540
  614.5 44.8 %copy-start.77 = (f32[2,64]{1,0:T(2,128)S(1)}, f32[2,64]{1,0:T(2,128)}, u32[]{:S(2)}) copy-start(f32[2,64]{1,0:T(2,128)} %copy-done.76) | copy-start | bytes 1540
  (39 other events, 61.7 us)
Sparse Core Ops, SparseCore 0:
  304.3 28.2 reduce-scatter.18
  393.7 26.3 reduce-scatter.20
  434.9 28.5 reduce-scatter.22
Sparse Core Ops, SparseCore 1:
  306.7 41.7 all-gather.2
  350.4 39.7 all-gather.4
  496.3 70.3 all-reduce.4
  570.0 62.5 reduce-scatter.36
  635.1 22.6 reduce-scatter.24
  661.7 63.1 reduce-scatter.30
  728.8 69.0 reduce-scatter.28
  801.8 69.1 reduce-scatter.26
  874.7 62.4 reduce-scatter.32
  941.1 62.3 reduce-scatter.34
where the time goes:
time: 1020 us; the launch traced here: 1010 us
  waiting for transfers between devices  501 us (49%)
  blocking collectives  320 us (31%)
  local copies, waits for them, and re-layouts  85.6 us (8%)
  matrix products  73.7 us (7%)
  between operations  16.4 us (2%)
  other arithmetic  13 us (1%)
    unnamed x17, waiting for transfers between devices  197 us
    psum x1, blocking collectives, per_device(): kv_sum, z_sum = lax.psum((kv_part, z_part), 'ctx')  96.4 us
    reduce_scatter x1, waiting for transfers between devices, per_device(): lax.psum_scatter(grad_up, ('shard', 'ctx'), scatter_dimension=0, tiled=True)  73.1 us
    reduce_scatter x1, waiting for transfers between devices, per_device(): lax.psum_scatter(grad_down, ('shard', 'ctx'), scatter_dimension=1, tiled=...  73 us
    mul x40, local copies, waits for them, and re-layouts, spread_rows(): wide = mask_low[:, None, :, None] * left[:, :, None, :]  51.8 us
    psum x1, blocking collectives, per_device(): lax.psum((grad_gain_attn, grad_shift_attn, grad_gain_ffn, grad_shift_ffn,...  40.8 us
    all_gather x1, waiting for transfers between devices, per_device(): lax.all_gather(w_down, ('shard', 'ctx'), axis=1, tiled=True)  38.5 us
    psum x1, waiting for transfers between devices, per_device(): lax.psum(kv_grad_part.astype(jnp.bfloat16), 'ctx').astype(jnp.float32)  33.9 us
  transfers between devices with their start and end apart: 13, of which 11 were waited for; matrix products, arithmetic and copies ran while one was open for 7% of the time, Pallas kernels for 0%

commit v1 on v0

--- a/solution.py
+++ b/solution.py
@@ -1,7 +1,9 @@
+import functools
 import jax
 import jax.numpy as jnp
 from jax import lax
 from jax.sharding import PartitionSpec as P
+from jax.lax import axis_index, axis_size, ppermute
 
 HEAD_DIM = 64
 FEATS = 256
@@ -11,6 +13,21 @@
 root_half = 0.7071067811865476
 inv_root_tau = 0.3989422804014327
 norm_eps = 1e-05
+
+
+def try_all_tiles_in(z_in, axis_id):
+    y2, row_out = (axis_size(axis_id), axis_index(axis_id))
+    right_arr, v1 = (z_in, 1)
+    while v1 < y2:
+        side_arr = ppermute(right_arr, axis_name=axis_id, perm=[(q, q ^ v1) for q in range(y2)])
+        h_now = jnp.concatenate([right_arr, side_arr], axis=1)
+        mid_arr = jnp.concatenate([side_arr, right_arr], axis=1)
+        right_arr = jnp.where(row_out & v1 == 0, h_now, mid_arr)
+        v1 = 2 * v1
+    return right_arr
+
+
+_divide_space = functools.partial(try_all_tiles_in, axis_id=("shard", "ctx"))
 
 
 def gelu_value(upper):
@@ -122,7 +139,7 @@
         lax.all_gather(w_key, ("shard", "ctx"), axis=0, tiled=True),
         lax.all_gather(w_value, ("shard", "ctx"), axis=0, tiled=True),
         lax.all_gather(w_up, ("shard", "ctx"), axis=0, tiled=True),
-        lax.all_gather(w_out, ("shard", "ctx"), axis=1, tiled=True),
+        _divide_space(w_out),
         lax.all_gather(w_down, ("shard", "ctx"), axis=1, tiled=True),
     )
     seq_count, row_share, width = inputs.shape

time: 1020 us -> 989 us (0.970)
  waiting for transfers between devices: 501 us -> 453 us
  local copies, waits for them, and re-layouts: 85.6 us -> 96.5 us
    reduce_scatter x4 -> x0, waiting for transfers between devices: 79.2 us -> none  [the longest x1 27.2 us: per_device(): lax.psum_scatter(jnp.einsum('scf,fd->csd', piece, full_out, preferred_ele...]
    unnamed x17 -> x21, waiting for transfers between devices: 197 us -> 234 us
    all_gather x1, waiting for transfers between devices: 38.5 us -> 26.5 us  [per_device(): lax.all_gather(w_down, ('shard', 'ctx'), axis=1, tiled=True)]
  transfers between devices with their start and end apart: 13 -> 16, of which waited for: 11 -> 12; matrix products, arithmetic and copies ran while one was open for 7% -> 13% of each run, Pallas kernels for 0% -> 0%
where the time goes in v1:
time: 989 us; the launch traced here: 981 us
  waiting for transfers between devices  453 us (46%)
  blocking collectives  319 us (32%)
  local copies, waits for them, and re-layouts  96.5 us (10%)
  matrix products  69.3 us (7%)
  other arithmetic  20.5 us (2%)
  between operations  16.9 us (2%)
    unnamed x21, waiting for transfers between devices  234 us
    psum x1, blocking collectives, per_device(): kv_sum, z_sum = lax.psum((kv_part, z_part), 'ctx')  96.9 us
    reduce_scatter x1, waiting for transfers between devices, per_device(): lax.psum_scatter(grad_up, ('shard', 'ctx'), scatter_dimension=0, tiled=True)  73 us
    reduce_scatter x1, waiting for transfers between devices, per_device(): lax.psum_scatter(grad_down, ('shard', 'ctx'), scatter_dimension=1, tiled=...  73 us
    mul x40, local copies, waits for them, and re-layouts, spread_rows(): wide = mask_low[:, None, :, None] * left[:, :, None, :]  51.4 us
    psum x1, blocking collectives, per_device(): lax.psum((grad_gain_attn, grad_shift_attn, grad_gain_ffn, grad_shift_ffn,...  40.6 us
    psum x1, waiting for transfers between devices, per_device(): lax.psum(kv_grad_part.astype(jnp.bfloat16), 'ctx').astype(jnp.float32)  37.1 us
    all_gather x1, blocking collectives, per_device(): lax.all_gather(w_key, ('shard', 'ctx'), axis=0, tiled=True)  32.2 us
  transfers between devices with their start and end apart: 16, of which 12 were waited for; matrix products, arithmetic and copies ran while one was open for 13% of the time, Pallas kernels for 0%

profile of v1, /device:TPU:0, one launch (start us, length us, event | category | flops | bytes accessed | tf_op | source)
XLA Modules:
  0.0 980.7 jit_solution(13319040716567500279)
XLA Ops:
  8.1 3.1 collective-permute-start
  11.2 8.8 all_gather.35
  20.0 32.2 %all_gather.36 = bf16[768,192]{1,0:T(8,128)(2,1)S(1)} all-gather(bf16[96,192]{1,0:T(8,128)(2,1)} %param.32), channel_id=1, replica_groups=mesh['shard'=2,'ctx'=4,'tp'=4] {'shard','ctx'}, dimensions={0}, use_global_device_ids=true | all-gather | bytes 331776 | tf_op jit(solution)/shard_map/all_gather | solution.py:139
  53.6 2.7 fusion.171
  57.5 31.7 %all_gather.37 = bf16[768,192]{1,0:T(8,128)(2,1)S(1)} all-gather(bf16[96,192]{1,0:T(8,128)(2,1)S(1)} %copy-done.46), channel_id=1, replica_groups=mesh['shard'=2,'ctx'=4,'tp'=4] {'shard','ctx'}, dimensions={0}, use_global_device_ids=true | all-gather | bytes 331776 | tf_op jit(solution)/shard_map/all_gather | solution.py:140
  92.0 2.1 convolution_bitcast_fusion.8
  94.0 20.6 %while.66 = (s32[]{:T(128)}, f32[2,3,2048,64]{2,3,1,0:T(8,128)}, bf16[2,256,8]{2,1,0:T(8,128)(2,1)S(1)}, bf16[2,256,3,256]{3,1,2,0:T(8,128)(2,1)}, bf16[2,256,3,64]{1,3,2,0:T(8,128)(2,1)}) while((s32[]{:T(128)}, f32[2,3,2048,64]{2,3,1,0:T(8,128)}, bf16[2,256,8]{2,1,0:T(8,128)(2,1)S(1)}, bf16[2,256,3,256]{3,1,2,0:T(8,128)(2,1)}, ...), condition=%wide.region_3.4_spmd.clone, body=%wide.region_2.3_spmd.sunk.clone | while | flops 207618048 | bytes 20427872 | solution.py:168
  95.1 2.1 mul.672
  97.2 4.2 mul.673
  102.3 2.0 fusion.245
  105.4 2.1 mul.672
  107.5 4.2 mul.673
  114.7 32.0 %all_gather.38 = bf16[768,192]{1,0:T(8,128)(2,1)S(1)} all-gather(bf16[96,192]{1,0:T(8,128)(2,1)S(1)} %copy-done.47), channel_id=1, replica_groups=mesh['shard'=2,'ctx'=4,'tp'=4] {'shard','ctx'}, dimensions={0}, use_global_device_ids=true | all-gather | bytes 331776 | tf_op jit(solution)/shard_map/all_gather | solution.py:138
  146.8 2.3 broadcast_multiply_fusion
  149.1 2.7 fusion.172
  153.1 96.9 %all-reduce.22 = (bf16[2,3,2048,64]{2,3,1,0:T(8,128)(2,1)}, f32[2,3,8,256]{3,2,1,0:T(8,128)S(1)}) all-reduce(f32[2,3,2048,64]{2,3,1,0:T(8,128)} %get-tuple-element.176, f32[2,3,8,256]{3,2,1,0:T(8,128)S(1)} %copy-done.44), channel_id=1, replica_groups=mesh['shard'=2,'ctx'=4,'tp'=4] {'ctx'}, use_global_device_ids=true, to_apply=%region_4.5 | all-reduce | flops 798720 | bytes 4816896 | tf_op jit(solution)/shard_map/psum | solution.py:170
  250.0 19.2 %while.67 = (s32[]{:T(128)}, f32[2,256,3,64]{1,3,2,0:T(8,128)}, bf16[2,3,2048,64]{2,3,1,0:T(8,128)(2,1)}, bf16[2,256,8]{2,1,0:T(8,128)(2,1)S(1)}, bf16[2,256,3,256]{3,1,2,0:T(8,128)(2,1)}) while((s32[]{:T(128)}, f32[2,256,3,64]{1,3,2,0:T(8,128)}, bf16[2,3,2048,64]{2,3,1,0:T(8,128)(2,1)}, bf16[2,256,8]{2,1,0:T(8,128)(2,1)S(1)}, ...), condition=%wide.region_6.7_spmd.clone, body=%wide.region_5.6_spmd.sunk.clone | while | flops 202899456 | bytes 31536224 | solution.py:172
  251.4 3.4 mul.678
  256.7 2.9 fusion.248
  261.1 3.4 mul.678
  266.3 2.8 fusion.248
  273.9 4.0 collective-permute-done.1
  278.2 5.1 collective-permute-done.2
  283.7 2.2 copy.129
  288.4 39.0 %all-reduce.15.cloned.1.call-done = f32[256,2,768]{2,1,0:T(2,128)} async-done(((f32[256,2,768]{2,1,0:T(2,128)}), f32[256,2,768]{2,1,0:T(2,128)}) %all-reduce.15.cloned.1.call-update) | async-done | bytes 1572880
  331.6 8.1 all_gather.39
  339.8 3.5 multiply_convert_fusion
  343.4 26.5 %all-gather.5.cloned.1.call-done = bf16[768,768]{0,1:T(8,128)(2,1)} async-done(((bf16[768,96]{0,1:T(8,128)(2,1)}), bf16[768,768]{0,1:T(8,128)(2,1)}) %all-gather.5.cloned.1.call-update) | async-done | bytes 1179664 | tf_op jit(solution)/shard_map/all_gather | solution.py:143
  369.9 2.1 convolution_bitcast_fusion.2
  372.0 2.5 copy.131
  374.5 41.3 %all-reduce.17.cloned.1.call-done = f32[256,2,768]{2,1,0:T(2,128)} async-done(((f32[256,2,768]{2,1,0:T(2,128)}), f32[256,2,768]{2,1,0:T(2,128)}) %all-reduce.17.cloned.1.call-update) | async-done | bytes 1572880
  421.3 8.4 all_gather.42
  433.2 2.4 copy.134
  437.1 32.0 %all_gather.44 = bf16[192,768]{0,1:T(8,128)(2,1)S(1)} all-gather(bf16[192,96]{0,1:T(8,128)(2,1)S(1)} %copy.135), channel_id=1, replica_groups=mesh['shard'=2,'ctx'=4,'tp'=4] {'shard','ctx'}, dimensions={1}, use_global_device_ids=true | all-gather | bytes 331776 | tf_op jit(solution)/shard_map/all_gather | solution.py:220
  471.3 7.8 all-reduce.19.cloned.1.call-done
  479.1 2.3 multiply_reduce_fusion.2
  482.6 8.2 all_gather.43
  492.9 20.1 %while.69 = (s32[]{:T(128)}, bf16[2,3,2048,64]{2,3,1,0:T(8,128)(2,1)}, bf16[2,256,8]{2,1,0:T(8,128)(2,1)S(1)}, bf16[2,256,3,256]{3,1,2,0:T(8,128)(2,1)}, bf16[2,256,3,64]{1,3,2,0:T(8,128)(2,1)}) while((s32[]{:T(128)}, bf16[2,3,2048,64]{2,3,1,0:T(8,128)(2,1)}, bf16[2,256,8]{2,1,0:T(8,128)(2,1)S(1)}, ...), condition=%wide.region_26.27_spmd.clone, body=%wide.region_25.26_spmd.sunk.clone | while | flops 207618048 | bytes 20427872 | solution.py:256
  494.0 2.1 mul.684
  496.0 4.2 mul.685
  504.0 2.1 mul.684
  506.1 4.2 mul.685
  514.9 7.0 while.68
  514.9 2.0 fusion.251
  521.9 2.5 fusion.173
  525.5 20.6 %psum.73 = bf16[2,3,8,256]{3,2,1,0:T(8,128)(2,1)S(1)} all-reduce(bf16[2,3,8,256]{3,2,1,0:T(8,128)(2,1)S(1)} %fusion.107), channel_id=1, replica_groups=mesh['shard'=2,'ctx'=4,'tp'=4] {'ctx'}, use_global_device_ids=true, to_apply=%region_31.32 | all-reduce | flops 12288 | bytes 49152 | tf_op jit(solution)/shard_map/psum | solution.py:262
  550.2 37.1 %all-reduce.13.cloned.1.call-done = bf16[2,3,2048,64]{2,3,1,0:T(8,128)(2,1)} async-done(((bf16[2,3,2048,64]{2,3,1,0:T(8,128)(2,1)}), bf16[2,3,2048,64]{2,3,1,0:T(8,128)(2,1)}) %all-reduce.13.cloned.1.call-update) | async-done | bytes 1572880 | tf_op jit(solution)/shard_map/psum | solution.py:261
  588.6 7.5 while.70
  588.6 2.3 fusion.257
  592.4 2.2 fusion.257
  600.9 19.5 %while.71 = (s32[]{:T(128)}, bf16[2,256,3,64]{1,3,2,0:T(8,128)(2,1)}, bf16[2,3,2048,64]{2,3,1,0:T(8,128)(2,1)}, bf16[2,256,8]{2,1,0:T(8,128)(2,1)S(1)}, bf16[2,256,3,256]{3,1,2,0:T(8,128)(2,1)}) while((s32[]{:T(128)}, bf16[2,256,3,64]{1,3,2,0:T(8,128)(2,1)}, bf16[2,3,2048,64]{2,3,1,0:T(8,128)(2,1)}, ...), condition=%wide.region_34.35_spmd.clone, body=%wide.region_33.34_spmd.sunk.clone | while | flops 202899456 | bytes 33109144 | solution.py:271
  602.4 3.4 mul.692
  607.8 2.2 fusion.260
  612.1 3.4 mul.692
  617.5 2.2 fusion.260
  620.4 2.5 fusion.75
  629.8 2.3 fusion.176
  633.5 2.2 fusion.175
  637.6 40.6 %all-reduce.4 = (f32[768]{0:T(1024)}, f32[768]{0:T(1024)}, f32[3072]{0:T(1024)S(1)}, f32[768]{0:T(1024)}, f32[768]{0:T(1024)}, /*index=5*/f32[768]{0:T(1024)}) all-reduce(f32[768]{0:T(1024)S(1)} %copy-done.54, f32[768]{0:T(1024)S(1)} %copy-done.55, ...), channel_id=1, replica_groups=mesh['shard'=2,'ctx'=4,'tp'=4] {'shard','ctx','tp'}, use_global_device_ids=true, to_apply=%region_41.42 | all-reduce | flops 6912 | bytes 55296 | tf_op jit(solution)/shard_map/psum | solution.py:315
  682.3 12.6 %reduce-scatter.19.cloned.1.call-done = f32[96,192]{1,0:T(8,128)} async-done(((f32[768,192]{1,0:T(8,128)}), f32[96,192]{1,0:T(8,128)}) %reduce-scatter.19.cloned.1.call-update) | async-done | bytes 73744
  694.8 66.3 %reduce-scatter.21.cloned.1.call-done = f32[96,192]{1,0:T(8,128)} async-done(((f32[768,192]{1,0:T(8,128)}), f32[96,192]{1,0:T(8,128)}) %reduce-scatter.21.cloned.1.call-update) | async-done | bytes 73744
  761.1 66.3 %reduce-scatter.23.cloned.1.call-done = f32[96,192]{1,0:T(8,128)} async-done(((f32[768,192]{1,0:T(8,128)}), f32[96,192]{1,0:T(8,128)}) %reduce-scatter.23.cloned.1.call-update) | async-done | bytes 73744
  827.4 73.0 %reduce-scatter.17.cloned.1.call-done = f32[768,96]{0,1:T(8,128)} async-done(((f32[768,768]{0,1:T(8,128)}), f32[768,96]{0,1:T(8,128)}) %reduce-scatter.17.cloned.1.call-update) | async-done | bytes 294928 | tf_op jit(solution)/shard_map/reduce_scatter | solution.py:308
  900.3 73.0 %reduce-scatter.15.cloned.1.call-done = f32[96,768]{1,0:T(8,128)} async-done(((f32[768,768]{1,0:T(8,128)}), f32[96,768]{1,0:T(8,128)}) %reduce-scatter.15.cloned.1.call-update) | async-done | bytes 294928 | tf_op jit(solution)/shard_map/reduce_scatter | solution.py:306
  (305 shorter events, 97.3 us)
Async XLA Ops:
  8.0 45.5 %copy-start = (f32[3,64,256]{2,1,0:T(8,128)S(1)}, f32[3,64,256]{2,1,0:T(8,128)}, u32[]{:S(2)}) copy-start(f32[3,64,256]{2,1,0:T(8,128)} %param.30) | copy-start | bytes 589828
  8.0 319.3 %all-reduce.15.cloned.1.call-start = ((), (), s32[]{:S(2)}) async-start(), calls=%async_computation.15 | async-start | bytes 3145728
  8.1 262.2 %collective-permute-start = (bf16[192,96]{1,0:T(8,128)(2,1)}, bf16[192,96]{1,0:T(8,128)(2,1)}, u32[]{:S(2)}, u32[]{:S(2)}) collective-permute-start(bf16[192,96]{1,0:T(8,128)(2,1)} %param.34), channel_id=1, source_target_pairs={{0,4},{4,0},{8,12},{12,8},{16,20},{20,16},{24,28},{28,24},{1,5},{5... | collective-permute-start | bytes 110600 | tf_op jit(solution)/shard_map/ppermute | solution.py:22
  20.0 69.2 %copy-start.4 = (bf16[2,256,768]{2,1,0:T(8,128)(2,1)}, bf16[2,256,768]{2,1,0:T(8,128)(2,1)S(1)}, u32[]{:S(2)}) copy-start(bf16[2,256,768]{2,1,0:T(8,128)(2,1)S(1)} %all_gather.35) | copy-start | bytes 2359300
  52.2 4.1 copy-start.14
  53.6 4.0 copy-start.46
  57.5 33.6 %copy-start.48 = (s32[2,256]{1,0:T(2,128)S(1)}, s32[2,256]{1,0:T(2,128)}, u32[]{:S(2)}) copy-start(s32[2,256]{1,0:T(2,128)} %param.29) | copy-start | bytes 6148
  94.0 20.6 %copy-start.47 = (bf16[96,192]{1,0:T(8,128)(2,1)S(1)}, bf16[96,192]{1,0:T(8,128)(2,1)}, u32[]{:S(2)}) copy-start(bf16[96,192]{1,0:T(8,128)(2,1)} %param.31) | copy-start | bytes 110596
  146.7 5.2 copy-start.16
  149.1 3.9 copy-start.44
  151.9 98.1 %copy-start.19 = (bf16[2,256,3,256]{1,3,0,2:T(8,128)(2,1)}, bf16[2,256,3,256]{1,3,0,2:T(8,128)(2,1)S(1)}, u32[]{:S(2)}) copy-start(bf16[2,256,3,256]{1,3,0,2:T(8,128)(2,1)S(1)} %get-tuple-element.412) | copy-start | bytes 2359300
  254.8 1.9 copy-start.1
  264.5 1.9 copy-start.1
  269.2 9.0 copy-start.41
  271.3 6.6 collective-permute-start.1
  278.1 5.2 collective-permute-start.2
  285.9 41.5 %copy-start.21 = (bf16[2,64,768]{2,1,0:T(8,128)(2,1)S(1)}, bf16[2,64,768]{2,1,0:T(8,128)(2,1)}, u32[]{:S(2)}) copy-start(bf16[2,64,768]{2,1,0:T(8,128)(2,1)} %param.28) | copy-start | bytes 589828
  285.9 44.2 %copy-start.45 = (f32[768]{0:T(1024)S(1)}, f32[768]{0:T(1024)}, u32[]{:S(2)}) copy-start(f32[768]{0:T(1024)} %param.35) | copy-start | bytes 9220
  285.9 44.2 %copy-start.49 = (f32[768]{0:T(1024)S(1)}, f32[768]{0:T(1024)}, u32[]{:S(2)}) copy-start(f32[768]{0:T(1024)} %param.36) | copy-start | bytes 9220
  285.9 53.9 %all-gather.3.cloned.1.call-start = ((), (), s32[]{:S(2)}) async-start(), calls=%async_computation.6 | async-start | bytes 1327104 | tf_op jit(solution)/shard_map/all_gather | solution.py:141
  286.5 83.4 %all-gather.5.cloned.1.call-start = ((), (), s32[]{:S(2)}) async-start(), calls=%async_computation.7 | async-start | bytes 1327104 | tf_op jit(solution)/shard_map/all_gather | solution.py:143
  287.1 128.8 %all-reduce.17.cloned.1.call-start = ((), (), s32[]{:S(2)}) async-start(), calls=%async_computation.16 | async-start | bytes 3145728
  331.6 8.2 copy-start.61
  339.8 3.6 copy-start.10
  343.4 28.6 %copy-start.24 = (bf16[512,768]{1,0:T(8,128)(2,1)}, bf16[512,768]{1,0:T(8,128)(2,1)S(1)}, u32[]{:S(2)}) copy-start(bf16[512,768]{1,0:T(8,128)(2,1)S(1)} %get-tuple-element.414) | copy-start | bytes 2359300
  374.4 41.4 %copy-start.56 = (f32[768]{0:T(1024)S(1)}, f32[768]{0:T(1024)}, u32[]{:S(2)}) copy-start(f32[768]{0:T(1024)} %param.40) | copy-start | bytes 9220
  374.4 43.2 %copy-start.38 = (bf16[2,64,768]{2,1,0:T(8,128)(2,1)S(1)}, bf16[2,64,768]{2,1,0:T(8,128)(2,1)}, u32[]{:S(2)}) copy-start(bf16[2,64,768]{2,1,0:T(8,128)(2,1)} %param.43) | copy-start | bytes 589828
  374.4 43.2 %copy-start.50 = (f32[768]{0:T(1024)S(1)}, f32[768]{0:T(1024)}, u32[]{:S(2)}) copy-start(f32[768]{0:T(1024)} %param.41) | copy-start | bytes 9220
  374.5 44.7 %copy-start.57 = (f32[768]{0:T(1024)S(1)}, f32[768]{0:T(1024)}, u32[]{:S(2)}) copy-start(f32[768]{0:T(1024)} %param.42) | copy-start | bytes 9220
  374.5 104.6 %all-reduce.19.cloned.1.call-start = ((), (), s32[]{:S(2)}) async-start(), calls=%async_computation.17 | async-start | bytes 3145728
  421.1 8.6 copy-start.60
  421.1 8.6 copy-start.63
  429.7 1.7 copy-start.22
  429.8 2.6 copy-start.59
  435.6 151.7 %all-reduce.13.cloned.1.call-start = ((), (), s32[]{:S(2)}) async-start(), calls=%async_computation.8 | async-start | bytes 3145728 | tf_op jit(solution)/shard_map/psum | solution.py:261
  482.6 9.2 copy-start.42
  513.0 2.0 copy-start.3
  513.0 165.8 %reduce-scatter.25.cloned.1.call-start = ((), (), s32[]{:S(2)}) async-start(), calls=%async_computation.14 | async-start | bytes 884736
  514.9 7.0 copy-start.8
  521.9 2.6 copy-start.20
  524.5 21.6 %copy-start.18 = (bf16[2,256,768]{2,1,0:T(8,128)(2,1)S(1)}, bf16[2,256,768]{2,1,0:T(8,128)(2,1)}, u32[]{:S(2)}) copy-start(bf16[2,256,768]{2,1,0:T(8,128)(2,1)} %copy.159) | copy-start | bytes 2359300
  524.5 21.6 %copy-start.37 = (bf16[24,8,2,256]{3,1,2,0:T(8,128)(2,1)S(1)}, bf16[24,8,2,256]{3,1,2,0:T(8,128)(2,1)}, u32[]{:S(2)}) copy-start(bf16[24,8,2,256]{3,1,2,0:T(8,128)(2,1)} %copy.231) | copy-start | bytes 589828
  524.5 22.9 %copy-start.34 = (f32[2,256,3,64]{1,3,2,0:T(8,128)S(1)}, f32[2,256,3,64]{1,3,2,0:T(8,128)}, u32[]{:S(2)}) copy-start(f32[2,256,3,64]{1,3,2,0:T(8,128)} %get-tuple-element.411) | copy-start | bytes 1179652
  548.6 40.1 %copy-start.29 = (bf16[2,256,3,64]{1,3,2,0:T(8,128)(2,1)}, bf16[2,256,3,64]{1,3,2,0:T(8,128)(2,1)S(1)}, u32[]{:S(2)}) copy-start(bf16[2,256,3,64]{1,3,2,0:T(8,128)(2,1)S(1)} %fusion.96) | copy-start | bytes 589828
  550.2 38.5 %copy-start.7 = (bf16[2,256,3,64]{1,3,2,0:T(8,128)(2,1)S(1)}, bf16[2,256,3,64]{1,3,2,0:T(8,128)(2,1)}, u32[]{:S(2)}) copy-start(bf16[2,256,3,64]{1,3,2,0:T(8,128)(2,1)} %get-tuple-element.795) | copy-start | bytes 589828
  550.2 130.2 %all-reduce.21.cloned.1.call-start = ((), (), s32[]{:S(2)}) async-start(), calls=%async_computation.18 | async-start | bytes 1572864
  588.6 7.5 copy-start.9
  596.1 2.0 copy-start.33
  605.8 2.0 copy-start.2
  615.5 2.0 copy-start.2
  623.0 1.8 copy-start.5
  623.0 1.8 copy-start.30
  624.7 1.7 copy-start.32
  624.7 70.1 %reduce-scatter.19.cloned.1.call-start = ((), (), s32[]{:S(2)}) async-start(), calls=%async_computation.11 | async-start | bytes 884736
  626.3 134.8 %reduce-scatter.21.cloned.1.call-start = ((), (), s32[]{:S(2)}) async-start(), calls=%async_computation.12 | async-start | bytes 884736
  627.9 199.5 %reduce-scatter.23.cloned.1.call-start = ((), (), s32[]{:S(2)}) async-start(), calls=%async_computation.13 | async-start | bytes 884736
  629.7 270.6 %reduce-scatter.17.cloned.1.call-start = ((), (), s32[]{:S(2)}) async-start(), calls=%async_computation.10 | async-start | bytes 2654208 | tf_op jit(solution)/shard_map/reduce_scatter | solution.py:308
  632.1 341.2 %reduce-scatter.15.cloned.1.call-start = ((), (), s32[]{:S(2)}) async-start(), calls=%async_computation.9 | async-start | bytes 2654208 | tf_op jit(solution)/shard_map/reduce_scatter | solution.py:306
  635.7 1.8 copy-start.51
  635.7 1.8 copy-start.52
  635.7 1.8 copy-start.53
  635.7 1.8 copy-start.54
  635.7 1.8 copy-start.55
  635.7 44.7 %copy-start.35 = (f32[2,64,768]{2,0,1:T(2,128)S(1)}, f32[2,64,768]{2,0,1:T(2,128)}, u32[]{:S(2)}) copy-start(f32[2,64,768]{2,0,1:T(2,128)} %get-tuple-element.393) | copy-start | bytes 1179652
  (22 other events, 24.5 us)
Sparse Core Ops, SparseCore 0:
  286.0 41.2 all-reduce.14
  374.6 41.2 all-reduce.16
  435.7 43.3 all-reduce.18
  513.1 74.1 all-reduce.12
  624.8 34.0 all-reduce.20
Sparse Core Ops, SparseCore 1:
  288.5 39.6 all-gather.2
  330.1 39.7 all-gather.4
  550.3 78.1 reduce-scatter.24
  632.4 62.4 reduce-scatter.18
  698.7 62.4 reduce-scatter.20
  765.0 62.3 reduce-scatter.22
  831.3 69.0 reduce-scatter.16
  904.2 69.0 reduce-scatter.14
